TPU v7x, 256 devices: a whole 4x4x8 slice. The times are simulated.
256 devices in a mesh: dp: 4 (over x), rad: 8 (over y, z_lo), azi: 8 (over z_hi, core).
Axes of the slice: x: 4, y: 4, z: 8 (z_hi: 4, z_lo: 2; z = z_hi * 2 + z_lo), core: 2. Of those that a mesh axis runs over, the one named last changes fastest.
Arguments:
- inputs: bfloat16 [4, 96, 32, 64, 256], P('dp', None, 'rad', 'azi'), may hold values from -6 to 6
- weight: bfloat16 [96, 2592], P('dp'), may hold values from -0.125 to 0.125
- bias: bfloat16 [96], P('dp'), may hold values from -3 to 3
- cotangent: bfloat16 [4, 96, 32, 64, 256], P('dp', None, 'rad', 'azi'), may hold values from -6 to 6
Outputs:
- output: bfloat16 [4, 96, 32, 64, 256], P('dp', None, 'rad', 'azi')
- input_grad: bfloat16 [4, 96, 32, 64, 256], P('dp', None, 'rad', 'azi')
- weight_grad: float32 [96, 2592], P('dp')
- bias_grad: float32 [96], P('dp')
All inputs are finite; a program needn't handle non-finite values.
Results may differ from a plain program's by a relative error of at most 0.015.
Values may be sent and summed in bfloat16 or wider, within the bound.
No kernel may reach another device: no remote copies, remote signals or barrier semaphores. Data moves between devices by JAX's collectives and lax.ppermute only.
A program may use at most 128 MiB of HBM per device.

v0:
```python
import jax
import jax.numpy as jnp
from jax import lax
from jax.sharding import PartitionSpec as P

inverse_scale = 1.0 / 1024.0


def with_halo(cells, sides, width):
    for axis, dim in sides:
        count = lax.axis_size(axis)
        head = lax.slice_in_dim(cells, 0, width, axis=dim)
        tail = lax.slice_in_dim(cells, cells.shape[dim] - width, cells.shape[dim], axis=dim)
        cells = jnp.concatenate(
            [
                lax.ppermute(tail, axis, [(i, (i + 1) % count) for i in range(count)]),
                cells,
                lax.ppermute(head, axis, [((i + 1) % count, i) for i in range(count)]),
            ],
            axis=dim,
        )
    return cells


def rim_fix(extended):
    rad_index = lax.axis_index("rad")
    rad_last = lax.axis_size("rad") - 1
    low_rim = jnp.where(rad_index > 0, extended[:, :, :1], jnp.zeros_like(extended[:, :, :1]))
    high_rim = jnp.where(
        rad_index < rad_last, extended[:, :, -1:], jnp.zeros_like(extended[:, :, -1:])
    )
    return jnp.concatenate([low_rim, extended[:, :, 1:-1], high_rim], axis=2)


def axial_pad(extended):
    return jnp.pad(extended, ((0, 0), (0, 0), (0, 0), (0, 0), (1, 1)))


def extend_input(field):
    extended = rim_fix(with_halo(field, (("rad", 2), ("azi", 3)), 1))
    return axial_pad(extended)


def extend_grad(field):
    extended = rim_fix(with_halo(field, (("rad", 2), ("azi", 3)), 1))
    return axial_pad(extended)


def convolve(left, right, numbers):
    return lax.conv_general_dilated(
        left,
        right,
        (1, 1, 1),
        "VALID",
        dimension_numbers=numbers,
        preferred_element_type=jnp.float32,
    )


def on_device(inputs, weight, bias, cotangent):
    channels = inputs.shape[1]
    full_weight, full_bias = (
        lax.all_gather(weight, "dp", axis=0, tiled=True),
        lax.all_gather(bias, "dp", axis=0, tiled=True),
    )
    out_rows = full_weight.shape[0]
    kernel_taps = full_weight.reshape(out_rows, 3, 3, 3, channels)
    kernel_fwd = kernel_taps.transpose(0, 4, 1, 2, 3)
    kernel_back = kernel_taps[:, ::-1, ::-1, ::-1, :].transpose(4, 0, 1, 2, 3)
    padded = extend_input(inputs)
    preact = convolve(padded, kernel_fwd, ("NCDHW", "OIDHW", "NCDHW"))
    preact = preact + full_bias.astype(jnp.float32)[None, :, None, None, None]
    gate_value = jax.nn.sigmoid(preact)
    output = (preact * gate_value).astype(jnp.bfloat16)
    delta_z = (
        cotangent.astype(jnp.float32) * gate_value * (1.0 + preact * (1.0 - gate_value))
    ).astype(jnp.bfloat16)
    delta_pad = extend_grad(delta_z)
    backward = convolve(delta_pad, kernel_back, ("NCDHW", "OIDHW", "NCDHW"))
    kernel_grad = convolve(padded, delta_z, ("CNDHW", "IODHW", "NCDHW"))
    weight_term = (
        kernel_grad.transpose(1, 2, 3, 4, 0).reshape(out_rows, 27 * channels) * inverse_scale
    )
    bias_term = jnp.sum(delta_z.astype(jnp.float32), axis=(0, 2, 3, 4)) * inverse_scale
    group_part = (
        lax.psum_scatter(
            weight_term.astype(jnp.bfloat16), "dp", scatter_dimension=0, tiled=True
        ).astype(jnp.float32),
        lax.psum_scatter(
            bias_term.astype(jnp.bfloat16), "dp", scatter_dimension=0, tiled=True
        ).astype(jnp.float32),
    )
    weight_grad, bias_grad = lax.psum((group_part[0], group_part[1]), ("rad", "azi"))
    return (output, backward.astype(jnp.bfloat16), weight_grad, bias_grad)


def solution(mesh):
    return jax.shard_map(
        on_device,
        mesh=mesh,
        in_specs=(
            P("dp", None, "rad", "azi", None),
            P("dp", None),
            P("dp"),
            P("dp", None, "rad", "azi", None),
        ),
        out_specs=(
            P("dp", None, "rad", "azi", None),
            P("dp", None, "rad", "azi", None),
            P("dp", None),
            P("dp"),
        ),
        check_vma=False,
    )
```

profile of v0, /device:TPU:2, one launch (start us, length us, event | category | flops | bytes accessed | tf_op | source)
XLA Modules:
  0.0 530.9 jit_solution(4180190173391444999)
XLA Ops:
  8.4 4.4 collective-permute-start.1
  12.8 9.5 %collective-permute-done.1 = bf16[1,96,1,8,256]{4,3,2,1,0:T(8,128)(2,1)S(1)} collective-permute-done((bf16[1,96,1,8,256]{4,3,2,1,0:T(8,128)(2,1)S(1)}, bf16[1,96,1,8,256]{4,3,2,1,0:T(8,128)(2,1)S(1)}, u32[]{:S(2)}, u32[]{:S(2)}) %collective-permute-start.1) | collective-permute-done | bytes 393248 | tf_op jit(solution)/shard_map/ppermute | solution.py:18
  22.3 8.0 %collective-permute-done = bf16[1,96,1,8,256]{4,3,2,1,0:T(8,128)(2,1)S(1)} collective-permute-done((bf16[1,96,1,8,256]{4,3,2,1,0:T(8,128)(2,1)S(1)}, bf16[1,96,1,8,256]{4,3,2,1,0:T(8,128)(2,1)S(1)}, u32[]{:S(2)}, u32[]{:S(2)}) %collective-permute-start) | collective-permute-done | bytes 393248 | tf_op jit(solution)/shard_map/ppermute | solution.py:16
  30.4 1.7 pad_maximum_fusion.3
  35.1 8.6 %all-reduce = bf16[96]{0:T(256)(128)(2,1)S(1)} all-reduce(bf16[96]{0:T(256)(128)(2,1)S(1)} %dynamic-update-slice), channel_id=1, replica_groups=mesh['dp'=4,'rad'=8,'azi'=8] {'dp'}, use_global_device_ids=true, to_apply=%add | all-reduce | flops 96 | bytes 384
  43.8 12.8 %all_gather.6 = bf16[96,2592]{1,0:T(8,128)(2,1)S(1)} all-gather(bf16[24,2592]{1,0:T(8,128)(2,1)} %param.5), channel_id=1, replica_groups=mesh['dp'=4,'rad'=8,'azi'=8] {'dp'}, dimensions={0}, use_global_device_ids=true | all-gather | bytes 622080 | tf_op jit(solution)/shard_map/all_gather | solution.py:63
  57.7 4.6 copy.69
  65.7 5.6 %collective-permute-done.3 = bf16[1,96,6,1,256]{4,1,3,2,0:T(8,128)(2,1)S(1)} collective-permute-done((bf16[1,96,6,1,256]{4,1,3,2,0:T(8,128)(2,1)S(1)}, bf16[1,96,6,1,256]{4,1,3,2,0:T(8,128)(2,1)S(1)}, u32[]{:S(2)}, u32[]{:S(2)}) %collective-permute-start.3) | collective-permute-done | bytes 294944 | tf_op jit(solution)/shard_map/ppermute | solution.py:18
  71.5 1.8 pad_maximum_fusion.1
  73.4 3.6 copy.88
  77.0 5.5 %pad.3.clone = bf16[96,6,10,1,264]{0,4,2,1,3:T(8,128)(2,1)} pad(bf16[96,6,10,1,256]{0,4,2,1,3:T(8,128)(2,1)} %copy.88, bf16[]{:T(256)} %constant.6.clone.1), padding=0_0x0_0x0_0x0_0x1_7 | pad | bytes 5990402 | tf_op jit(solution)/shard_map/concatenate | solution.py:32
  82.5 7.2 %reshape.21 = bf16[96,6,10,1,8,33]{0,5,4,2,1,3:T(8,128)(2,1)} reshape(bf16[96,6,10,1,264]{0,4,2,1,3:T(8,128)(2,1)} %pad.3.clone) | data formatting | bytes 6082560 | tf_op jit(solution)/shard_map/conv_general_dilated | solution.py:50
  89.7 3.1 copy.66
  92.9 17.9 %add_divide_fusion = (f32[4,8,8,33,96]{4,2,3,1,0:T(8,128)S(1)}, bf16[4,8,8,33,96]{4,2,3,1,0:T(8,128)(2,1)}, f32[4,8,8,33,96]{4,2,3,1,0:T(8,128)S(1)}) fusion(f32[96]{0:T(128)S(1)} %convert_element_type.36, pred[8,33]{0,1:T(8,128)(4,1)S(1)} %copy-done.8, bf16[96,3,3,3,96]{0,4,3,2,1:T(8,128)(2,1)S(1)} %bitcast.55, ...), kind=kOutput, calls=%fused_computation.6 | convolution fusion | flops 4222052352 | bytes 11810952 | tf_op jit(solution)/shard_map/conv_general_dilated | solution.py:50
  113.2 1.6 convert_reduce_fusion
  117.4 2.0 collective-permute-start.4
  119.4 16.3 %copy.83 = bf16[1,96,6,10,256]{1,0,4,3,2:T(2,128)(2,1)} copy(bf16[1,96,6,10,256]{4,1,3,2,0:T(8,128)(2,1)} %get-tuple-element.25) | data formatting | bytes 5898240 | tf_op jit(solution)/shard_map/concatenate | solution.py:32
  135.8 63.2 %fusion.28 = bf16[96,3,3,3,96]{0,4,3,2,1:T(8,128)(2,1)S(1)} fusion(bf16[1,96,6,10,256]{1,0,4,3,2:T(2,128)(2,1)} %copy.83, bf16[1,96,4,8,256]{1,3,4,2,0:T(8,128)(2,1)S(1)} %get-tuple-element.19), kind=kOutput, calls=%fused_computation.38 | convolution fusion | flops 4066744320 | bytes 5019648 | tf_op jit(solution)/shard_map/transpose | solution.py:82
  200.7 4.6 copy.86
  206.4 1.5 copy.75
  208.0 1.5 copy.74
  210.3 1.6 copy-done
  213.6 3.8 collective-permute-start.7
  218.0 11.4 %all-reduce.2 = bf16[96]{0:T(256)(128)(2,1)S(1)} all-reduce(bf16[96]{0:T(256)(128)(2,1)S(1)} %multiply_convert_fusion.1), channel_id=3, replica_groups=mesh['dp'=4,'rad'=8,'azi'=8] {'dp'}, use_global_device_ids=true, to_apply=%region_3.4.clone | all-reduce | flops 96 | bytes 384
  229.5 3.7 copy.78
  234.3 3.7 copy.89
  238.0 5.4 %pad.5.clone = bf16[96,6,10,1,264]{0,4,2,1,3:T(8,128)(2,1)} pad(bf16[96,6,10,1,256]{0,4,2,1,3:T(8,128)(2,1)} %copy.89, bf16[]{:T(256)} %constant.6.clone.1), padding=0_0x0_0x0_0x0_0x1_7 | pad | bytes 5990402 | tf_op jit(solution)/shard_map/concatenate | solution.py:32
  243.4 7.2 %reshape.28 = bf16[96,6,10,1,8,33]{0,5,4,2,1,3:T(8,128)(2,1)} reshape(bf16[96,6,10,1,264]{0,4,2,1,3:T(8,128)(2,1)} %pad.5.clone) | data formatting | bytes 6082560 | tf_op jit(solution)/shard_map/conv_general_dilated | solution.py:50
  250.7 3.1 copy.81
  253.9 15.8 %select_convert_fusion = bf16[4,8,8,33,96]{4,2,3,1,0:T(8,128)(2,1)S(1)} fusion(pred[8,33]{0,1:T(8,128)(4,1)S(1)} %copy-done.9, bf16[96,3,3,3,96]{0,4,3,2,1:T(8,128)(2,1)S(1)} %bitcast.56, bf16[96,6,10,1,7,2]{0,4,5,2,1,3:T(8,128)(2,1)S(1)} %slice.76, bf16[96,6,10,1,8,33]{0,4,5,2,1,3:T(8,128)(2,1)S(1)} %copy.81), kind=kOutput, calls=%fused_computation.3 | convolution fusion | flops 4215564288 | bytes 5322504 | tf_op jit(solution)/shard_map/conv_general_dilated | solution.py:50
  270.1 3.0 copy.87
  273.1 250.6 %all-reduce.5 = (f32[24,2592]{1,0:T(8,128)}, f32[24]{0:T(128)}) all-reduce(bf16[24,2592]{1,0:T(8,128)(2,1)} %reduce-scatter.4.cloned.1.call-done, f32[24]{0:T(128)S(1)} %dynamic-slice_convert_fusion), channel_id=1, replica_groups=mesh['dp'=4,'rad'=8,'azi'=8] {'rad','azi'}, use_global_device_ids=true, to_apply=%region_1.2 | all-reduce | flops 62232 | bytes 373440 | tf_op jit(solution)/shard_map/psum | solution.py:93
  (68 shorter events, 20.0 us)
Async XLA Ops:
  7.2 265.9 %reduce-scatter.4.cloned.1.call-start = ((), (), s32[]{:S(2)}) async-start(), calls=%async_computation.1 | async-start | bytes 645120
  8.4 13.9 %collective-permute-start.1 = (bf16[1,96,1,8,256]{4,3,2,1,0:T(8,128)(2,1)S(1)}, bf16[1,96,1,8,256]{4,3,2,1,0:T(8,128)(2,1)S(1)}, u32[]{:S(2)}, u32[]{:S(2)}) collective-permute-start(bf16[1,96,1,8,256]{4,3,2,1,0:T(8,128)(2,1)S(1)} %get-tuple-element.36), channel_id=1, source_target_pairs={{8,0},{16,8},{24,16},{32,24},{40,32},{48,40},{56,48},{0,56},{9,1},... | collective-permute-start | bytes 1179656 | tf_op jit(solution)/shard_map/ppermute | solution.py:18
  12.8 20.8 %copy-start.5 = (u32[256]{0:T(256)S(1)}, u32[256]{0:T(256)}, u32[]{:S(2)}) copy-start(u32[256]{0:T(256)} %constant.33) | copy-start | bytes 3076
  12.8 22.0 %copy-start.7 = (bf16[24]{0:T(256)(128)(2,1)S(1)}, bf16[24]{0:T(256)(128)(2,1)}, u32[]{:S(2)}) copy-start(bf16[24]{0:T(256)(128)(2,1)} %param.6) | copy-start | bytes 148
  12.8 17.5 %collective-permute-start = (bf16[1,96,1,8,256]{4,3,2,1,0:T(8,128)(2,1)S(1)}, bf16[1,96,1,8,256]{4,3,2,1,0:T(8,128)(2,1)S(1)}, u32[]{:S(2)}, u32[]{:S(2)}) collective-permute-start(bf16[1,96,1,8,256]{4,3,2,1,0:T(8,128)(2,1)S(1)} %get-tuple-element.35), channel_id=1, source_target_pairs={{0,8},{8,16},{16,24},{24,32},{32,40},{40,48},{48,56},{56,0},{1,9},... | collective-permute-start | bytes 1179656 | tf_op jit(solution)/shard_map/ppermute | solution.py:16
  33.6 30.3 %collective-permute-start.2 = (bf16[1,96,6,1,256]{4,1,3,2,0:T(8,128)(2,1)}, bf16[1,96,6,1,256]{4,1,3,2,0:T(8,128)(2,1)}, u32[]{:S(2)}, u32[]{:S(2)}) collective-permute-start(bf16[1,96,6,1,256]{4,1,3,2,0:T(8,128)(2,1)} %copy.97), channel_id=1, source_target_pairs={{0,1},{1,2},{2,3},{3,4},{4,5},{5,6},{6,7},{7,0},{8,9},{9,10},{10,1... | collective-permute-start | bytes 884744 | tf_op jit(solution)/shard_map/ppermute | solution.py:16
  63.0 8.3 %collective-permute-start.3 = (bf16[1,96,6,1,256]{4,1,3,2,0:T(8,128)(2,1)S(1)}, bf16[1,96,6,1,256]{4,1,3,2,0:T(8,128)(2,1)S(1)}, u32[]{:S(2)}, u32[]{:S(2)}) collective-permute-start(bf16[1,96,6,1,256]{4,1,3,2,0:T(8,128)(2,1)S(1)} %copy.98), channel_id=1, source_target_pairs={{1,0},{2,1},{3,2},{4,3},{5,4},{6,5},{7,6},{0,7},{9,8},{10,9},{11,1... | collective-permute-start | bytes 884744 | tf_op jit(solution)/shard_map/ppermute | solution.py:18
  89.7 3.2 copy-start.3
  89.7 3.2 copy-start.8
  111.6 1.6 copy-start.1
  116.2 90.3 %collective-permute-start.5 = (bf16[1,96,1,8,256]{4,3,2,1,0:T(8,128)(2,1)}, bf16[1,96,1,8,256]{4,3,2,1,0:T(8,128)(2,1)}, u32[]{:S(2)}, u32[]{:S(2)}) collective-permute-start(bf16[1,96,1,8,256]{4,3,2,1,0:T(8,128)(2,1)} %copy.73), channel_id=1, source_target_pairs={{8,0},{16,8},{24,16},{32,24},{40,32},{48,40},{56,48},{0,56},{9,1},... | collective-permute-start | bytes 1179656 | tf_op jit(solution)/shard_map/ppermute | solution.py:18
  117.4 90.6 %collective-permute-start.4 = (bf16[1,96,1,8,256]{4,3,2,1,0:T(8,128)(2,1)}, bf16[1,96,1,8,256]{4,3,2,1,0:T(8,128)(2,1)}, u32[]{:S(2)}, u32[]{:S(2)}) collective-permute-start(bf16[1,96,1,8,256]{4,3,2,1,0:T(8,128)(2,1)} %copy.72), channel_id=1, source_target_pairs={{0,8},{8,16},{16,24},{24,32},{32,40},{40,48},{48,56},{56,0},{1,9},... | collective-permute-start | bytes 1179656 | tf_op jit(solution)/shard_map/ppermute | solution.py:16
  135.8 63.2 %copy-start.2 = (bf16[4,8,8,33,96]{4,2,3,1,0:T(8,128)(2,1)S(1)}, bf16[4,8,8,33,96]{4,2,3,1,0:T(8,128)(2,1)}, u32[]{:S(2)}) copy-start(bf16[4,8,8,33,96]{4,2,3,1,0:T(8,128)(2,1)} %get-tuple-element.21) | copy-start | bytes 4866052
  210.3 1.6 copy-start
  211.9 6.1 %copy-start.6 = (f32[96]{0:T(128)S(1)}, f32[96]{0:T(128)}, u32[]{:S(2)}) copy-start(f32[96]{0:T(128)} %get-tuple-element.18) | copy-start | bytes 1156
  213.6 19.7 %collective-permute-start.7 = (bf16[1,96,6,1,256]{4,1,3,2,0:T(8,128)(2,1)S(1)}, bf16[1,96,6,1,256]{4,1,3,2,0:T(8,128)(2,1)S(1)}, u32[]{:S(2)}, u32[]{:S(2)}) collective-permute-start(bf16[1,96,6,1,256]{4,1,3,2,0:T(8,128)(2,1)S(1)} %copy.77), channel_id=1, source_target_pairs={{1,0},{2,1},{3,2},{4,3},{5,4},{6,5},{7,6},{0,7},{9,8},{10,9},{11,1... | collective-permute-start | bytes 884744 | tf_op jit(solution)/shard_map/ppermute | solution.py:18
  217.9 15.4 %collective-permute-start.6 = (bf16[1,96,6,1,256]{4,1,3,2,0:T(8,128)(2,1)S(1)}, bf16[1,96,6,1,256]{4,1,3,2,0:T(8,128)(2,1)S(1)}, u32[]{:S(2)}, u32[]{:S(2)}) collective-permute-start(bf16[1,96,6,1,256]{4,1,3,2,0:T(8,128)(2,1)S(1)} %copy.76), channel_id=1, source_target_pairs={{0,1},{1,2},{2,3},{3,4},{4,5},{5,6},{6,7},{7,0},{8,9},{9,10},{10,1... | collective-permute-start | bytes 884744 | tf_op jit(solution)/shard_map/ppermute | solution.py:16
  250.7 3.2 copy-start.4
  250.7 3.2 copy-start.9
Sparse Core Ops, SparseCore 0:
  206.6 25.3 reduce-scatter.3
where the time goes:
time: 537 us; the launch traced here: 531 us
  blocking collectives  283 us (53%)
  matrix products  96.9 us (18%)
  local copies, waits for them, and re-layouts  93.1 us (17%)
  waiting for transfers between devices  23.2 us (4%)
  between operations  16.1 us (3%)
  starting transfers between devices  11.3 us (2%)
  other arithmetic  6.9 us (1%)
    psum x1, blocking collectives, on_device(): lax.psum((group_part[0], group_part[1]), ('rad', 'azi'))  251 us
    transpose x1, matrix products, on_device(): kernel_grad.transpose(1, 2, 3, 4, 0).reshape(out_rows, 27 * channels)  63.2 us
    conv_general_dilated x2, matrix products, convolve(): lax.conv_general_dilated(left, right, (1, 1, 1), 'VALID', dimension_numbe...  33.7 us
    concatenate x3, local copies, waits for them, and re-layouts, rim_fix(): return jnp.concatenate([low_rim, extended[:, :, 1:-1], high_rim], axis=2)  27.2 us
    unnamed x32, local copies, waits for them, and re-layouts  25.5 us
    conv_general_dilated x6, local copies, waits for them, and re-layouts, convolve(): lax.conv_general_dilated(left, right, (1, 1, 1), 'VALID', dimension_numbe...  20.8 us
    unnamed x2, blocking collectives  20.1 us
    ppermute x4, waiting for transfers between devices, with_halo(): lax.ppermute(head, axis, [((i + 1) % count, i) for i in range(count)])  15.1 us
  transfers between devices with their start and end apart: 9, of which 3 were waited for; matrix products, arithmetic and copies ran while one was open for 28% of the time, Pallas kernels for 0%

commit v1 on v0

--- a/solution.py
+++ b/solution.py
@@ -90,7 +90,7 @@
             bias_term.astype(jnp.bfloat16), "dp", scatter_dimension=0, tiled=True
         ).astype(jnp.float32),
     )
-    weight_grad, bias_grad = lax.psum((group_part[0], group_part[1]), ("rad", "azi"))
+    weight_grad, bias_grad = lax.psum(lax.psum((group_part[0], group_part[1]), "rad"), "azi")
     return (output, backward.astype(jnp.bfloat16), weight_grad, bias_grad)
 
 

time: 537 us -> 396 us (0.74)
  blocking collectives: 283 us -> 85.8 us
  waiting for transfers between devices: 23.2 us -> 75.1 us
    psum x1 -> x2, blocking collectives: 251 us -> 53 us  [the longest x1 38.3 us: on_device(): lax.psum((group_part[0], group_part[1]), 'rad')]
    psum x0 -> x1, waiting for transfers between devices: none -> 51.9 us  [on_device(): lax.psum(lax.psum((group_part[0], group_part[1]), 'rad'), 'azi')]
    unnamed x32 -> x33, local copies, waits for them, and re-layouts: 25.5 us -> 28.8 us
  transfers between devices with their start and end apart: 9 -> 10, of which waited for: 3 -> 4; matrix products, arithmetic and copies ran while one was open for 28% -> 38% of each run, Pallas kernels for 0% -> 0%
where the time goes in v1:
time: 396 us; the launch traced here: 390 us
  local copies, waits for them, and re-layouts  97.8 us (25%)
  matrix products  96.9 us (24%)
  blocking collectives  85.8 us (22%)
  waiting for transfers between devices  75.1 us (19%)
  between operations  16.2 us (4%)
  starting transfers between devices  11.3 us (3%)
  other arithmetic  6.91 us (2%)
    transpose x1, matrix products, on_device(): kernel_grad.transpose(1, 2, 3, 4, 0).reshape(out_rows, 27 * channels)  63.2 us
    psum x1, waiting for transfers between devices, on_device(): lax.psum(lax.psum((group_part[0], group_part[1]), 'rad'), 'azi')  51.9 us
    psum x1, blocking collectives, on_device(): lax.psum((group_part[0], group_part[1]), 'rad')  38.3 us
    conv_general_dilated x2, matrix products, convolve(): lax.conv_general_dilated(left, right, (1, 1, 1), 'VALID', dimension_numbe...  33.7 us
    unnamed x33, local copies, waits for them, and re-layouts  28.8 us
    concatenate x3, local copies, waits for them, and re-layouts, rim_fix(): return jnp.concatenate([low_rim, extended[:, :, 1:-1], high_rim], axis=2)  27.3 us
    conv_general_dilated x6, local copies, waits for them, and re-layouts, convolve(): lax.conv_general_dilated(left, right, (1, 1, 1), 'VALID', dimension_numbe...  20.8 us
    unnamed x2, blocking collectives  20.1 us
  transfers between devices with their start and end apart: 10, of which 4 were waited for; matrix products, arithmetic and copies ran while one was open for 38% of the time, Pallas kernels for 0%

profile of v1, /device:TPU:2, one launch (start us, length us, event | category | flops | bytes accessed | tf_op | source)
XLA Modules:
  0.0 390.1 jit_solution(7782347793337828013)
XLA Ops:
  8.4 4.4 %collective-permute-start.1 = (bf16[1,96,1,8,256]{4,3,2,1,0:T(8,128)(2,1)S(1)}, bf16[1,96,1,8,256]{4,3,2,1,0:T(8,128)(2,1)S(1)}, u32[]{:S(2)}, u32[]{:S(2)}) collective-permute-start(bf16[1,96,1,8,256]{4,3,2,1,0:T(8,128)(2,1)S(1)} %get-tuple-element.36), channel_id=1, source_target_pairs={{8,0},{16,8},{24,16},{32,24},{40,32},{48,40},{56,48},{0,56},{9,1},... | collective-permute-start | bytes 1179656 | tf_op jit(solution)/shard_map/ppermute | solution.py:18
  12.8 9.5 %collective-permute-done.1 = bf16[1,96,1,8,256]{4,3,2,1,0:T(8,128)(2,1)S(1)} collective-permute-done((bf16[1,96,1,8,256]{4,3,2,1,0:T(8,128)(2,1)S(1)}, bf16[1,96,1,8,256]{4,3,2,1,0:T(8,128)(2,1)S(1)}, u32[]{:S(2)}, u32[]{:S(2)}) %collective-permute-start.1) | collective-permute-done | bytes 393248 | tf_op jit(solution)/shard_map/ppermute | solution.py:18
  22.3 8.0 %collective-permute-done = bf16[1,96,1,8,256]{4,3,2,1,0:T(8,128)(2,1)S(1)} collective-permute-done((bf16[1,96,1,8,256]{4,3,2,1,0:T(8,128)(2,1)S(1)}, bf16[1,96,1,8,256]{4,3,2,1,0:T(8,128)(2,1)S(1)}, u32[]{:S(2)}, u32[]{:S(2)}) %collective-permute-start) | collective-permute-done | bytes 393248 | tf_op jit(solution)/shard_map/ppermute | solution.py:16
  30.4 1.7 pad_maximum_fusion.3
  35.1 8.6 %all-reduce = bf16[96]{0:T(256)(128)(2,1)S(1)} all-reduce(bf16[96]{0:T(256)(128)(2,1)S(1)} %dynamic-update-slice), channel_id=1, replica_groups=mesh['dp'=4,'rad'=8,'azi'=8] {'dp'}, use_global_device_ids=true, to_apply=%add | all-reduce | flops 96 | bytes 384
  43.8 12.8 %all_gather.6 = bf16[96,2592]{1,0:T(8,128)(2,1)S(1)} all-gather(bf16[24,2592]{1,0:T(8,128)(2,1)} %param.5), channel_id=1, replica_groups=mesh['dp'=4,'rad'=8,'azi'=8] {'dp'}, dimensions={0}, use_global_device_ids=true | all-gather | bytes 622080 | tf_op jit(solution)/shard_map/all_gather | solution.py:63
  57.7 4.6 %copy.69 = bf16[1,96,4,8,256]{1,3,4,2,0:T(8,128)(2,1)} copy(bf16[1,96,4,8,256]{4,3,2,1,0:T(8,128)(2,1)} %param.7) | data formatting | bytes 3145728 | tf_op args[3]
  65.7 5.6 %collective-permute-done.3 = bf16[1,96,6,1,256]{4,1,3,2,0:T(8,128)(2,1)S(1)} collective-permute-done((bf16[1,96,6,1,256]{4,1,3,2,0:T(8,128)(2,1)S(1)}, bf16[1,96,6,1,256]{4,1,3,2,0:T(8,128)(2,1)S(1)}, u32[]{:S(2)}, u32[]{:S(2)}) %collective-permute-start.3) | collective-permute-done | bytes 294944 | tf_op jit(solution)/shard_map/ppermute | solution.py:18
  71.6 1.8 pad_maximum_fusion.1
  73.4 3.7 copy.88
  77.1 5.5 %pad.3.clone = bf16[96,6,10,1,264]{0,4,2,1,3:T(8,128)(2,1)} pad(bf16[96,6,10,1,256]{0,4,2,1,3:T(8,128)(2,1)} %copy.88, bf16[]{:T(256)} %constant.6.clone.1), padding=0_0x0_0x0_0x0_0x1_7 | pad | bytes 5990402 | tf_op jit(solution)/shard_map/concatenate | solution.py:32
  82.6 7.2 %reshape.21 = bf16[96,6,10,1,8,33]{0,5,4,2,1,3:T(8,128)(2,1)} reshape(bf16[96,6,10,1,264]{0,4,2,1,3:T(8,128)(2,1)} %pad.3.clone) | data formatting | bytes 6082560 | tf_op jit(solution)/shard_map/conv_general_dilated | solution.py:50
  89.8 3.1 copy.66
  93.0 18.0 %add_divide_fusion = (f32[4,8,8,33,96]{4,2,3,1,0:T(8,128)S(1)}, bf16[4,8,8,33,96]{4,2,3,1,0:T(8,128)(2,1)}, f32[4,8,8,33,96]{4,2,3,1,0:T(8,128)S(1)}) fusion(f32[96]{0:T(128)S(1)} %convert_element_type.36, pred[8,33]{0,1:T(8,128)(4,1)S(1)} %copy-done.8, bf16[96,3,3,3,96]{0,4,3,2,1:T(8,128)(2,1)S(1)} %bitcast.55, ...), kind=kOutput, calls=%fused_computation.6 | convolution fusion | flops 4222052352 | bytes 11810952 | tf_op jit(solution)/shard_map/conv_general_dilated | solution.py:50
  117.5 2.0 collective-permute-start.4
  119.5 16.4 %copy.83 = bf16[1,96,6,10,256]{1,0,4,3,2:T(2,128)(2,1)} copy(bf16[1,96,6,10,256]{4,1,3,2,0:T(8,128)(2,1)} %get-tuple-element.25) | data formatting | bytes 5898240 | tf_op jit(solution)/shard_map/concatenate | solution.py:32
  135.9 63.2 %fusion.28 = bf16[96,3,3,3,96]{0,4,3,2,1:T(8,128)(2,1)S(1)} fusion(bf16[1,96,6,10,256]{1,0,4,3,2:T(2,128)(2,1)} %copy.83, bf16[1,96,4,8,256]{1,3,4,2,0:T(8,128)(2,1)S(1)} %get-tuple-element.19), kind=kOutput, calls=%fused_computation.38 | convolution fusion | flops 4066744320 | bytes 5019648 | tf_op jit(solution)/shard_map/transpose | solution.py:82
  200.9 4.6 %copy.86 = bf16[1,96,4,8,256]{4,3,2,1,0:T(8,128)(2,1)} copy(bf16[1,96,4,8,256]{1,3,4,2,0:T(8,128)(2,1)} %slice_bitcast_fusion.3) | data formatting | bytes 3145728
  210.5 1.6 copy-done
  213.8 3.8 collective-permute-start.7
  218.2 11.4 %all-reduce.2 = bf16[96]{0:T(256)(128)(2,1)S(1)} all-reduce(bf16[96]{0:T(256)(128)(2,1)S(1)} %multiply_convert_fusion.1), channel_id=3, replica_groups=mesh['dp'=4,'rad'=8,'azi'=8] {'dp'}, use_global_device_ids=true, to_apply=%region_4.5.clone | all-reduce | flops 96 | bytes 384
  229.7 3.7 copy.78
  234.5 3.7 copy.89
  238.2 5.4 %pad.5.clone = bf16[96,6,10,1,264]{0,4,2,1,3:T(8,128)(2,1)} pad(bf16[96,6,10,1,256]{0,4,2,1,3:T(8,128)(2,1)} %copy.89, bf16[]{:T(256)} %constant.6.clone.1), padding=0_0x0_0x0_0x0_0x1_7 | pad | bytes 5990402 | tf_op jit(solution)/shard_map/concatenate | solution.py:32
  243.6 7.2 %reshape.28 = bf16[96,6,10,1,8,33]{0,5,4,2,1,3:T(8,128)(2,1)} reshape(bf16[96,6,10,1,264]{0,4,2,1,3:T(8,128)(2,1)} %pad.5.clone) | data formatting | bytes 6082560 | tf_op jit(solution)/shard_map/conv_general_dilated | solution.py:50
  250.8 3.1 copy.81
  254.0 15.8 %select_convert_fusion = bf16[4,8,8,33,96]{4,2,3,1,0:T(8,128)(2,1)S(1)} fusion(pred[8,33]{0,1:T(8,128)(4,1)S(1)} %copy-done.9, bf16[96,3,3,3,96]{0,4,3,2,1:T(8,128)(2,1)S(1)} %bitcast.56, bf16[96,6,10,1,7,2]{0,4,5,2,1,3:T(8,128)(2,1)S(1)} %slice.76, bf16[96,6,10,1,8,33]{0,4,5,2,1,3:T(8,128)(2,1)S(1)} %copy.81), kind=kOutput, calls=%fused_computation.3 | convolution fusion | flops 4215564288 | bytes 5322504 | tf_op jit(solution)/shard_map/conv_general_dilated | solution.py:50
  270.1 38.3 %all-reduce.8 = (f32[24,2592]{1,0:T(8,128)}, f32[24]{0:T(128)S(1)}) all-reduce(bf16[24,2592]{1,0:T(8,128)(2,1)} %reduce-scatter.4.cloned.1.call-done, f32[24]{0:T(128)S(1)} %dynamic-slice_convert_fusion), channel_id=1, replica_groups=mesh['dp'=4,'rad'=8,'azi'=8] {'rad'}, use_global_device_ids=true, to_apply=%region_1.2 | all-reduce | flops 62232 | bytes 373440 | tf_op jit(solution)/shard_map/psum | solution.py:93
  309.9 4.6 %copy.87 = bf16[1,96,4,8,256]{4,3,2,1,0:T(8,128)(2,1)} copy(bf16[1,96,4,8,256]{1,3,4,2,0:T(8,128)(2,1)} %slice_bitcast_fusion.2) | data formatting | bytes 3145728
  314.6 14.7 %psum.31 = f32[24]{0:T(128)} all-reduce(f32[24]{0:T(128)S(1)} %get-tuple-element.17), channel_id=1, replica_groups=mesh['dp'=4,'rad'=8,'azi'=8] {'azi'}, use_global_device_ids=true, to_apply=%region_6.7 | all-reduce | flops 24 | bytes 192 | tf_op jit(solution)/shard_map/psum | solution.py:93
  329.3 51.9 %all-reduce.7.cloned.1.call-done = f32[24,2592]{1,0:T(8,128)} async-done(((f32[24,2592]{1,0:T(8,128)}), f32[24,2592]{1,0:T(8,128)}) %all-reduce.7.cloned.1.call-update) | async-done | bytes 248848 | tf_op jit(solution)/shard_map/psum | solution.py:93
  381.1 1.7 copy.106
  (73 shorter events, 26.1 us)
Async XLA Ops:
  7.2 263.0 %reduce-scatter.4.cloned.1.call-start = ((), (), s32[]{:S(2)}) async-start(), calls=%async_computation.2 | async-start | bytes 645120
  8.4 13.9 %collective-permute-start.1 = (bf16[1,96,1,8,256]{4,3,2,1,0:T(8,128)(2,1)S(1)}, bf16[1,96,1,8,256]{4,3,2,1,0:T(8,128)(2,1)S(1)}, u32[]{:S(2)}, u32[]{:S(2)}) collective-permute-start(bf16[1,96,1,8,256]{4,3,2,1,0:T(8,128)(2,1)S(1)} %get-tuple-element.36), channel_id=1, source_target_pairs={{8,0},{16,8},{24,16},{32,24},{40,32},{48,40},{56,48},{0,56},{9,1},... | collective-permute-start | bytes 1179656 | tf_op jit(solution)/shard_map/ppermute | solution.py:18
  12.8 20.8 %copy-start.5 = (u32[256]{0:T(256)S(1)}, u32[256]{0:T(256)}, u32[]{:S(2)}) copy-start(u32[256]{0:T(256)} %constant.33) | copy-start | bytes 3076
  12.8 22.0 %copy-start.7 = (bf16[24]{0:T(256)(128)(2,1)S(1)}, bf16[24]{0:T(256)(128)(2,1)}, u32[]{:S(2)}) copy-start(bf16[24]{0:T(256)(128)(2,1)} %param.6) | copy-start | bytes 148
  12.8 17.5 %collective-permute-start = (bf16[1,96,1,8,256]{4,3,2,1,0:T(8,128)(2,1)S(1)}, bf16[1,96,1,8,256]{4,3,2,1,0:T(8,128)(2,1)S(1)}, u32[]{:S(2)}, u32[]{:S(2)}) collective-permute-start(bf16[1,96,1,8,256]{4,3,2,1,0:T(8,128)(2,1)S(1)} %get-tuple-element.35), channel_id=1, source_target_pairs={{0,8},{8,16},{16,24},{24,32},{32,40},{40,48},{48,56},{56,0},{1,9},... | collective-permute-start | bytes 1179656 | tf_op jit(solution)/shard_map/ppermute | solution.py:16
  33.6 30.3 %collective-permute-start.2 = (bf16[1,96,6,1,256]{4,1,3,2,0:T(8,128)(2,1)}, bf16[1,96,6,1,256]{4,1,3,2,0:T(8,128)(2,1)}, u32[]{:S(2)}, u32[]{:S(2)}) collective-permute-start(bf16[1,96,6,1,256]{4,1,3,2,0:T(8,128)(2,1)} %copy.97), channel_id=1, source_target_pairs={{0,1},{1,2},{2,3},{3,4},{4,5},{5,6},{6,7},{7,0},{8,9},{9,10},{10,1... | collective-permute-start | bytes 884744 | tf_op jit(solution)/shard_map/ppermute | solution.py:16
  63.0 8.3 %collective-permute-start.3 = (bf16[1,96,6,1,256]{4,1,3,2,0:T(8,128)(2,1)S(1)}, bf16[1,96,6,1,256]{4,1,3,2,0:T(8,128)(2,1)S(1)}, u32[]{:S(2)}, u32[]{:S(2)}) collective-permute-start(bf16[1,96,6,1,256]{4,1,3,2,0:T(8,128)(2,1)S(1)} %copy.98), channel_id=1, source_target_pairs={{1,0},{2,1},{3,2},{4,3},{5,4},{6,5},{7,6},{0,7},{9,8},{10,9},{11,1... | collective-permute-start | bytes 884744 | tf_op jit(solution)/shard_map/ppermute | solution.py:18
  89.8 3.2 copy-start.3
  89.8 3.2 copy-start.8
  111.7 1.6 copy-start.1
  116.3 90.4 %collective-permute-start.5 = (bf16[1,96,1,8,256]{4,3,2,1,0:T(8,128)(2,1)}, bf16[1,96,1,8,256]{4,3,2,1,0:T(8,128)(2,1)}, u32[]{:S(2)}, u32[]{:S(2)}) collective-permute-start(bf16[1,96,1,8,256]{4,3,2,1,0:T(8,128)(2,1)} %copy.73), channel_id=1, source_target_pairs={{8,0},{16,8},{24,16},{32,24},{40,32},{48,40},{56,48},{0,56},{9,1},... | collective-permute-start | bytes 1179656 | tf_op jit(solution)/shard_map/ppermute | solution.py:18
  117.5 90.7 %collective-permute-start.4 = (bf16[1,96,1,8,256]{4,3,2,1,0:T(8,128)(2,1)}, bf16[1,96,1,8,256]{4,3,2,1,0:T(8,128)(2,1)}, u32[]{:S(2)}, u32[]{:S(2)}) collective-permute-start(bf16[1,96,1,8,256]{4,3,2,1,0:T(8,128)(2,1)} %copy.72), channel_id=1, source_target_pairs={{0,8},{8,16},{16,24},{24,32},{32,40},{40,48},{48,56},{56,0},{1,9},... | collective-permute-start | bytes 1179656 | tf_op jit(solution)/shard_map/ppermute | solution.py:16
  135.9 63.2 %copy-start.2 = (bf16[4,8,8,33,96]{4,2,3,1,0:T(8,128)(2,1)S(1)}, bf16[4,8,8,33,96]{4,2,3,1,0:T(8,128)(2,1)}, u32[]{:S(2)}) copy-start(bf16[4,8,8,33,96]{4,2,3,1,0:T(8,128)(2,1)} %get-tuple-element.21) | copy-start | bytes 4866052
  206.6 174.5 %all-reduce.7.cloned.1.call-start = ((), (), s32[]{:S(2)}) async-start(), calls=%async_computation.1 | async-start | bytes 516096 | tf_op jit(solution)/shard_map/psum | solution.py:93
  210.5 1.6 copy-start
  212.1 6.1 %copy-start.6 = (f32[96]{0:T(128)S(1)}, f32[96]{0:T(128)}, u32[]{:S(2)}) copy-start(f32[96]{0:T(128)} %get-tuple-element.18) | copy-start | bytes 1156
  213.8 19.7 %collective-permute-start.7 = (bf16[1,96,6,1,256]{4,1,3,2,0:T(8,128)(2,1)S(1)}, bf16[1,96,6,1,256]{4,1,3,2,0:T(8,128)(2,1)S(1)}, u32[]{:S(2)}, u32[]{:S(2)}) collective-permute-start(bf16[1,96,6,1,256]{4,1,3,2,0:T(8,128)(2,1)S(1)} %copy.77), channel_id=1, source_target_pairs={{1,0},{2,1},{3,2},{4,3},{5,4},{6,5},{7,6},{0,7},{9,8},{10,9},{11,1... | collective-permute-start | bytes 884744 | tf_op jit(solution)/shard_map/ppermute | solution.py:18
  218.1 15.4 %collective-permute-start.6 = (bf16[1,96,6,1,256]{4,1,3,2,0:T(8,128)(2,1)S(1)}, bf16[1,96,6,1,256]{4,1,3,2,0:T(8,128)(2,1)S(1)}, u32[]{:S(2)}, u32[]{:S(2)}) collective-permute-start(bf16[1,96,6,1,256]{4,1,3,2,0:T(8,128)(2,1)S(1)} %copy.76), channel_id=1, source_target_pairs={{0,1},{1,2},{2,3},{3,4},{4,5},{5,6},{6,7},{7,0},{8,9},{9,10},{10,1... | collective-permute-start | bytes 884744 | tf_op jit(solution)/shard_map/ppermute | solution.py:16
  250.8 3.2 copy-start.4
  250.8 3.2 copy-start.9
Sparse Core Ops, SparseCore 0:
  206.7 25.3 reduce-scatter.3
  308.6 72.5 all-reduce.6
